TPU v7x, 512 devices: a whole 4x8x8 slice. The times are simulated.
512 devices in a mesh: samp: 32 (over x, z), blk: 16 (over y, core).
Axes of the slice: x: 4, y: 8, z: 8, core: 2. Of those that a mesh axis runs over, the one named last changes fastest.
Arguments:
- dosages: int32 [49152, 8192], P('samp', 'blk'), may hold values from 0 to 2, as said below
- new_dosages: int32 [49152, 2048], P('samp', 'blk'), may hold values from 0 to 2, as said below
- traits: float32 [64, 49152], P(None, 'samp'), may hold values from -40 to 40
- shrink: float32 [5], replicated, may hold values from 0.5 to 5
Outputs:
- residual: float32 [5, 64, 49152], P(None, 'blk', 'samp')
- scores: float32 [5, 64, 2048], P(None, None, 'blk')
Inputs may be any that keep to these rules, and one draw needn't show every extreme that they name: `dosages`: codes of haplotype pairs, with linkage along neighbouring variants. `new_dosages`: codes of haplotype pairs, with linkage along neighbouring variants.
All inputs are finite; a program needn't handle non-finite values.
Results may differ from a plain program's by a relative error of at most 0.0053.
Values may be sent and summed in bfloat16 or wider, within the bound.
No kernel may reach another device: no remote copies, remote signals or barrier semaphores. Data moves between devices by JAX's collectives and lax.ppermute only.
A program may use at most 64 MiB of HBM per device.

v0:
```python
import jax
import jax.numpy as jnp
from jax import lax
from jax.sharding import Mesh, PartitionSpec as P

RIDGE = 5
SAMP = ("x", "z")
BLK = ("y", "core")
FACTORS = {32: (4, 8), 16: (8, 2), 4: (2, 2)}
EPS = 1e-05
F32 = jnp.float32
BF16 = jnp.bfloat16


def dot(a, b, contract, precision=None):
    return lax.dot_general(
        a, b, (contract, ((), ())), precision=precision, preferred_element_type=F32
    )


def rounded(values):
    return lax.reduce_precision(values, 8, 7)


def column_stats(shifted_sum, shifted_sq, count):
    mean = (shifted_sum + count) / count
    var = (shifted_sq + 2.0 * shifted_sum + count) / count - mean * mean
    return (mean, 1.0 / jnp.sqrt(var + EPS))


def scaled(codes, mean, inv):
    return ((codes.astype(F32) - mean) * inv).astype(BF16)


def affine(shifted_sum, shifted_sq, mean, inv, count):
    low, mid, high = (rounded((code - mean) * inv) for code in (0.0, 1.0, 2.0))
    n_low = (shifted_sq - shifted_sum) * 0.5
    n_high = (shifted_sq + shifted_sum) * 0.5
    n_mid = count - shifted_sq
    value_mean = (n_low * low + n_mid * mid + n_high * high) / count
    pairs = n_low * n_mid + n_mid * n_high + 4.0 * n_low * n_high
    slopes = (
        n_low * n_mid * (mid - low)
        + n_mid * n_high * (high - mid)
        + 2.0 * n_low * n_high * (high - low)
    )
    slope = jnp.where(pairs > 0.0, slopes / jnp.maximum(pairs, 1.0), inv)
    square = (n_low * low * low + n_mid * mid * mid + n_high * high * high) / count
    return (value_mean, slope, square)


def chebyshev_coefficients(lam, bound):
    centre = lam + bound / 2.0
    half = bound / 2.0
    sig = centre / half
    q0 = 1.0 / sig
    d0 = 1.0 / centre
    r1a, r1b = (1.0 - lam * d0, -d0)
    q1 = 1.0 / (2.0 * sig - q0)
    step = 2.0 * q1 / half
    d1a, d1b = (q1 * q0 * d0 + step * r1a, step * r1b)
    r2a = r1a - lam * d1a
    r2b = r1b - d1a - lam * d1b
    r2c = -d1b
    q2 = 1.0 / (2.0 * sig - q1)
    step = 2.0 * q2 / half
    d2a, d2b, d2c = (q2 * q1 * d1a + step * r2a, q2 * q1 * d1b + step * r2b, step * r2c)
    return (d0 + d1a + d2a, d1b + d2b, d2c)


def shards(dosages, new_dosages, traits, shrink):
    rows, width = dosages.shape
    fresh_width = new_dosages.shape[1]
    trait_count = traits.shape[0]
    samp, blk = (lax.axis_size(SAMP), lax.axis_size(BLK))
    depth, cores, zs = (lax.axis_size("y"), lax.axis_size("core"), lax.axis_size("z"))
    count = float(rows * samp)
    half_width = width // 2
    share_rows = half_width // samp
    share = trait_count // blk
    columns = RIDGE * trait_count
    codes = (dosages - 1).astype(BF16)
    codes_f = (dosages - 1).astype(F32)
    new_f = (new_dosages - 1).astype(F32)
    trait_bf = traits.astype(BF16)
    parts = (
        jnp.sum(codes_f, axis=0),
        jnp.sum(codes_f * codes_f, axis=0),
        jnp.sum(new_f, axis=0),
        jnp.sum(new_f * new_f, axis=0),
        jnp.sum(trait_bf.astype(F32), axis=1),
    )
    sizes = [p.shape[0] for p in parts]
    slots = share_rows * 256
    sums = jnp.pad(jnp.concatenate(parts), (0, slots - sum(sizes))).reshape(share_rows, 256)
    first, second = (codes[:, :half_width], codes[:, half_width:])
    over_rows = ((0,), (0,))
    gram_top = dot(first, codes, over_rows)
    gram_low = dot(second, second, over_rows)
    cross = dot(codes, trait_bf, ((0,), (1,)))
    wide = 3 * half_width
    payload = jnp.concatenate(
        [gram_top, gram_low, cross[:half_width], cross[half_width:]], axis=1
    ).reshape(samp, share_rows, wide + 2 * trait_count)
    payload = jnp.concatenate(
        [payload, jnp.broadcast_to(sums[None], (samp, share_rows, 256))], axis=2
    )
    chunk = jnp.sum(lax.all_to_all(payload, SAMP, 0, 0, tiled=True), axis=0)
    totals = chunk[:, wide + 2 * trait_count :].reshape(slots)
    pieces, at = ([], 0)
    for size in sizes:
        pieces.append(totals[at : at + size])
        at += size
    code_sum, code_sq, new_sum, new_sq, trait_sum = pieces
    mean, inv = column_stats(code_sum, code_sq, count)
    value_mean, slope, square = affine(code_sum, code_sq, mean, inv, count)
    start = lax.axis_index(SAMP) * share_rows

    def own(vector, offset):
        return lax.dynamic_slice(vector, (start + offset,), (share_rows,))[:, None]

    def centred(product, offset, column_from):
        sums_i, slope_i, value_i = (own(v, offset) for v in (code_sum, slope, value_mean))
        out = (
            slope_i
            * slope[None, column_from:]
            * (product / count - sums_i / count * (code_sum[None, column_from:] / count))
        )
        out = out + value_i * value_mean[None, column_from:]
        row = start + offset + lax.broadcasted_iota(jnp.int32, out.shape, 0)
        column = column_from + lax.broadcasted_iota(jnp.int32, out.shape, 1)
        return jnp.where(row == column, 0.0, out)

    def centred_cross(product, offset):
        sums_i, slope_i, value_i = (own(v, offset) for v in (code_sum, slope, value_mean))
        trait_mean = trait_sum[None, :] / count
        return slope_i * (product / count - sums_i / count * trait_mean) + value_i * trait_mean

    rhs_rows = jnp.concatenate(
        [
            centred_cross(chunk[:, wide : wide + trait_count], 0),
            centred_cross(chunk[:, wide + trait_count : wide + 2 * trait_count], half_width),
        ],
        axis=1,
    )
    rhs_high = rounded(rhs_rows)
    own_rows = jnp.concatenate(
        [
            centred(chunk[:, :width], 0, 0),
            centred(chunk[:, width:wide], half_width, half_width),
            rhs_high,
            rhs_rows - rhs_high,
        ],
        axis=1,
    ).astype(BF16)
    every = lax.all_to_all(
        jnp.broadcast_to(own_rows[None], (samp, *own_rows.shape)), SAMP, 0, 0, tiled=True
    ).reshape(half_width, own_rows.shape[1])
    top_left, top_right = (every[:, :half_width], every[:, half_width:width])
    low_right = every[:, width:wide]
    gram = jnp.concatenate(
        [
            jnp.concatenate([top_left, top_right], axis=1),
            jnp.concatenate([top_right.T, low_right], axis=1),
        ],
        axis=0,
    )
    bound = jnp.max(jnp.sum(jnp.abs(gram.astype(F32)), axis=0) + square)
    rhs_parts = every[:, wide:].reshape(half_width, 2, 2, trait_count)
    rhs_parts = rhs_parts.transpose(1, 3, 2, 0).reshape(2 * trait_count, width)

    def apply_gram(high, low, whole):
        out = dot(jnp.concatenate([high, low], axis=0), gram, ((1,), (0,)))
        return out[:trait_count] + out[trait_count:] + square[None, :] * whole

    high, low = (rhs_parts[:trait_count], rhs_parts[trait_count:])
    rhs = high.astype(F32) + low.astype(F32)
    once = apply_gram(high, low, rhs)
    once_high = rounded(once)
    twice = apply_gram(once_high.astype(BF16), (once - once_high).astype(BF16), once)
    coefficients = chebyshev_coefficients(shrink, bound)
    row = lax.broadcasted_iota(jnp.int32, (columns, 3 * trait_count), 0)
    column = lax.broadcasted_iota(jnp.int32, (columns, 3 * trait_count), 1)
    side, in_side = (row // (columns // cores), row % (columns // cores))
    place, in_place = (in_side // (RIDGE * share), in_side % (RIDGE * share))
    ridge, in_share = (in_place // share, in_place % share)
    core = lax.rem(lax.axis_index("core") + 1 + side, cores)
    trait = (place * cores + core) * share + in_share
    mixing = jnp.zeros((columns, 3 * trait_count), F32)
    for power in range(3):
        for r in range(RIDGE):
            mixing = jnp.where(
                (ridge == r) & (column == trait + power * trait_count),
                coefficients[power][r],
                mixing,
            )
    weights = dot(
        mixing, jnp.concatenate([rhs, once, twice], axis=0), ((1,), (0,)), lax.Precision.HIGHEST
    ).astype(BF16)
    standard = scaled(dosages, mean, inv)
    new_mean, new_inv = column_stats(new_sum, new_sq, count)
    fresh = scaled(new_dosages, new_mean, new_inv)
    half_columns = columns // cores
    along = ((1,), (1,))
    sent = dot(weights[:half_columns], standard, along).astype(BF16)
    kept = dot(weights[half_columns:], standard, along)
    arrived = lax.ppermute(sent, "core", [(0, 1), (1, 0)])
    paired = (kept + arrived.astype(F32)).astype(BF16).reshape(depth, RIDGE * share, rows)
    summed = lax.all_to_all(paired, "y", 0, 0, tiled=True)
    pred = jnp.sum(summed.astype(F32), axis=0).reshape(RIDGE, share, rows)
    own_traits = lax.dynamic_slice_in_dim(traits, lax.axis_index(BLK) * share, share, 0)
    residual = own_traits[None] - pred
    res_bf = lax.all_gather(
        residual.astype(BF16).reshape(RIDGE * share, rows), BLK, axis=0, tiled=True
    )
    raw_part = dot(res_bf, fresh, ((1,), (0,)))
    res_float = res_bf.astype(F32)
    squares = jnp.sum(res_float * res_float, axis=1).reshape(zs, 1, columns // zs)
    squares = jnp.pad(squares, ((0, 0), (0, 7), (0, fresh_width - columns // zs)))
    ends = jnp.concatenate([raw_part.reshape(zs, columns // zs, fresh_width), squares], axis=1)
    ends = jnp.sum(lax.all_to_all(ends, "z", 0, 0, tiled=True), axis=0)
    ends = lax.psum(ends, "x")
    raw, sum_sq = (ends[: columns // zs], ends[columns // zs, : columns // zs])
    scores = raw / jnp.sqrt(count * (sum_sq / count + EPS))[:, None]
    scores = lax.all_to_all(
        jnp.broadcast_to(scores[None], (zs, *scores.shape)), "z", 0, 0, tiled=True
    )
    scores = scores.reshape(blk, RIDGE, share, fresh_width).transpose(1, 0, 2, 3)
    return (residual, scores.reshape(RIDGE, trait_count, fresh_width))


def solution(mesh):
    samp, blk = (FACTORS[mesh.shape["samp"]], FACTORS[mesh.shape["blk"]])
    grid = Mesh(mesh.devices.reshape(*samp, *blk), SAMP + BLK)
    return jax.shard_map(
        shards,
        mesh=grid,
        in_specs=(P(SAMP, BLK), P(SAMP, BLK), P(None, SAMP), P()),
        out_specs=(P(None, BLK, SAMP), P(None, None, BLK)),
        check_vma=False,
    )
```

profile of v0, /device:TPU:8, one launch (start us, length us, event | category | flops | bytes accessed | tf_op | source)
XLA Modules:
  0.0 220.9 jit_solution(13262179598304185275)
XLA Ops:
  0.6 2.3 %add_convert_fusion = bf16[1536,512]{1,0:T(8,128)(2,1)S(1)} fusion(s32[1536,512]{1,0:T(8,128)} %param.4), kind=kLoop, calls=%fused_computation.3 | loop fusion | flops 1572864 | bytes 4718592 | tf_op jit(solution)/shard_map/convert_element_type | solution.py:82
  3.0 1.4 fusion.2
  6.6 2.1 fusion.119
  9.8 1.3 constant_dynamic-update-slice_fusion.4
  11.1 1.3 constant_dynamic-update-slice_fusion.3
  13.6 1.3 constant_dynamic-update-slice_fusion.1
  14.9 1.3 constant_dynamic-update-slice_fusion
  16.9 1.4 maximum_bitcast_fusion
  19.4 13.3 %all-to-all-start = ((f32[32,8,1152]{2,1,0:T(8,128)}), f32[32,8,1152]{2,1,0:T(8,128)}, u32[]{:S(2)}, u32[]{:S(2)}) async-start(f32[32,8,1152]{2,1,0:T(8,128)} %pad_maximum_fusion), calls=%async_computation | async-start | bytes 2359296 | tf_op jit(solution)/shard_map/all_to_all | solution.py:108
  33.7 30.3 %all-to-all-done = f32[32,8,1152]{2,1,0:T(8,128)} async-done(((f32[32,8,1152]{2,1,0:T(8,128)}), f32[32,8,1152]{2,1,0:T(8,128)}, u32[]{:S(2)}, u32[]{:S(2)}) %all-to-all-start) | async-done | bytes 1179680 | tf_op jit(solution)/shard_map/all_to_all | solution.py:108
  64.0 2.0 reduce_sum.97
  71.6 5.3 %all-to-all-start.1 = ((bf16[32,8,1024]{2,1,0:T(8,128)(2,1)}), bf16[32,8,1024]{2,1,0:T(8,128)(2,1)}, u32[]{:S(2)}, u32[]{:S(2)}) async-start(bf16[32,8,1024]{2,1,0:T(8,128)(2,1)} %broadcast_in_dim.108), calls=%async_computation.1 | async-start | bytes 1048576 | tf_op jit(solution)/shard_map/all_to_all | solution.py:156
  78.7 14.7 %all-to-all-done.1 = bf16[32,8,1024]{2,1,0:T(8,128)(2,1)} async-done(((bf16[32,8,1024]{2,1,0:T(8,128)(2,1)}), bf16[32,8,1024]{2,1,0:T(8,128)(2,1)}, u32[]{:S(2)}, u32[]{:S(2)}) %all-to-all-start.1) | async-done | bytes 524320 | tf_op jit(solution)/shard_map/all_to_all | solution.py:156
  93.5 1.8 fusion.170
  95.3 1.7 concatenate.57
  96.9 1.7 copy.34
  100.4 1.4 fusion.150
  105.7 1.7 copy.28
  108.5 1.3 fusion.111
  110.6 11.3 %convolution_convert_fusion.1 = bf16[320,512]{1,0:T(8,128)(2,1)S(1)} fusion(f32[64,512]{1,0:T(8,128)S(1)} %fusion.109, f32[64,512]{1,0:T(8,128)S(1)} %get-tuple-element.14, f32[64,512]{1,0:T(8,128)S(1)} %get-tuple-element.20, f32[]{:T(128)} %bitcast.18, f32[]{:T(128)} %bitcast.17, f32[]{:T(128)} %bitcast.16, f32[]{:T(128)} %bitcast.15, f32[]{:T(128)} %bitcast.14, ...), kind=kOutput, calls=%fused_computation.6 | convolution fusion | flops 383008768 | bytes 726720 | tf_op jit(solution)/shard_map/dot_general | solution.py:16
  122.5 1.9 collective-permute-start
  124.5 1.8 collective-permute-done
  126.3 1.5 add_convert_fusion.1
  127.8 2.0 reshape.255
  129.8 7.5 %all-to-all-start.2 = ((bf16[8,20,1536]{2,1,0:T(8,128)(2,1)}), bf16[8,20,1536]{2,1,0:T(8,128)(2,1)S(1)}, u32[]{:S(2)}, u32[]{:S(2)}) async-start(bf16[8,20,1536]{2,1,0:T(8,128)(2,1)} %reshape.255), calls=%async_computation.2 | async-start | bytes 1179648 | tf_op jit(solution)/shard_map/all_to_all | solution.py:209
  138.1 16.9 %all-to-all-done.2 = bf16[8,20,1536]{2,1,0:T(8,128)(2,1)S(1)} async-done(((bf16[8,20,1536]{2,1,0:T(8,128)(2,1)}), bf16[8,20,1536]{2,1,0:T(8,128)(2,1)S(1)}, u32[]{:S(2)}, u32[]{:S(2)}) %all-to-all-start.2) | async-done | bytes 491552 | tf_op jit(solution)/shard_map/all_to_all | solution.py:209
  155.2 19.1 %all-gather = bf16[16,20,1536]{2,1,0:T(8,128)(2,1)S(1)} all-gather(bf16[1,20,1536]{2,1,0:T(8,128)(2,1)S(1)} %fusion.121), channel_id=1, replica_groups=mesh['x'=4,'z'=8,'y'=8,'core'=2] {'y','core'}, dimensions={0}, use_global_device_ids=true | all-gather | bytes 1044480 | tf_op jit(solution)/shard_map/all_gather | solution.py:213
  176.0 4.2 %all-to-all-start.3 = ((f32[8,48,128]{2,1,0:T(8,128)}), f32[8,48,128]{2,1,0:T(8,128)S(1)}, u32[]{:S(2)}, u32[]{:S(2)}) async-start(f32[8,48,128]{2,1,0:T(8,128)} %select_maximum_fusion), calls=%async_computation.3 | async-start | bytes 393216 | tf_op jit(solution)/shard_map/all_to_all | solution.py:221
  180.3 11.0 %all-to-all-done.3 = f32[8,48,128]{2,1,0:T(8,128)S(1)} async-done(((f32[8,48,128]{2,1,0:T(8,128)}), f32[8,48,128]{2,1,0:T(8,128)S(1)}, u32[]{:S(2)}, u32[]{:S(2)}) %all-to-all-start.3) | async-done | bytes 196640 | tf_op jit(solution)/shard_map/all_to_all | solution.py:221
  191.3 15.4 %psum.7 = f32[48,128]{1,0:T(8,128)S(1)} all-reduce(f32[48,128]{1,0:T(8,128)S(1)} %reduce_sum.102), channel_id=1, replica_groups=mesh['x'=4,'z'=8,'y'=8,'core'=2] {'x'}, use_global_device_ids=true, to_apply=%region_11.12 | all-reduce | flops 6144 | bytes 49152 | tf_op jit(solution)/shard_map/psum | solution.py:222
  207.4 3.4 %all-to-all-start.4 = ((f32[8,40,128]{2,1,0:T(8,128)}), f32[8,40,128]{2,1,0:T(8,128)S(1)}, u32[]{:S(2)}, u32[]{:S(2)}) async-start(f32[8,40,128]{2,1,0:T(8,128)} %broadcast_in_dim.125), calls=%async_computation.4 | async-start | bytes 327680 | tf_op jit(solution)/shard_map/all_to_all | solution.py:225
  211.5 8.7 %all-to-all-done.4 = f32[8,40,128]{2,1,0:T(8,128)S(1)} async-done(((f32[8,40,128]{2,1,0:T(8,128)}), f32[8,40,128]{2,1,0:T(8,128)S(1)}, u32[]{:S(2)}, u32[]{:S(2)}) %all-to-all-start.4) | async-done | bytes 163872 | tf_op jit(solution)/shard_map/all_to_all | solution.py:225
  (99 shorter events, 27.3 us)
Async XLA Ops:
  3.0 2.5 %copy-start.1 = (bf16[1536,512]{1,0:T(8,128)(2,1)}, bf16[1536,512]{1,0:T(8,128)(2,1)S(1)}, u32[]{:S(2)}) copy-start(bf16[1536,512]{1,0:T(8,128)(2,1)S(1)} %add_convert_fusion) | copy-start | bytes 4718596
  3.0 2.6 %copy-start = (s32[1536,512]{1,0:T(8,128)S(1)}, s32[1536,512]{1,0:T(8,128)}, u32[]{:S(2)}) copy-start(s32[1536,512]{1,0:T(8,128)} %param.4) | copy-start | bytes 9437188
  5.6 1.0 copy-start.4
  6.6 2.9 %copy-start.2 = (s32[1536,128]{1,0:T(8,128)S(1)}, s32[1536,128]{1,0:T(8,128)}, u32[]{:S(2)}) copy-start(s32[1536,128]{1,0:T(8,128)} %param.5) | copy-start | bytes 2359300
  19.4 44.6 %all-to-all-start = ((f32[32,8,1152]{2,1,0:T(8,128)}), f32[32,8,1152]{2,1,0:T(8,128)}, u32[]{:S(2)}, u32[]{:S(2)}) async-start(f32[32,8,1152]{2,1,0:T(8,128)} %pad_maximum_fusion), calls=%async_computation | async-start | bytes 2359296 | tf_op jit(solution)/shard_map/all_to_all | solution.py:108
  68.5 0.6 copy-start.8
  71.6 21.8 %all-to-all-start.1 = ((bf16[32,8,1024]{2,1,0:T(8,128)(2,1)}), bf16[32,8,1024]{2,1,0:T(8,128)(2,1)}, u32[]{:S(2)}, u32[]{:S(2)}) async-start(bf16[32,8,1024]{2,1,0:T(8,128)(2,1)} %broadcast_in_dim.108), calls=%async_computation.1 | async-start | bytes 1048576 | tf_op jit(solution)/shard_map/all_to_all | solution.py:156
  107.4 2.6 %copy-start.5 = (bf16[256,512]{1,0:T(8,128)(2,1)S(1)}, bf16[256,512]{1,0:T(8,128)(2,1)}, u32[]{:S(2)}) copy-start(bf16[256,512]{1,0:T(8,128)(2,1)} %concatenate.57) | copy-start | bytes 786436
  107.4 2.6 %copy-start.6 = (bf16[256,256]{0,1:T(8,128)(2,1)S(1)}, bf16[256,256]{0,1:T(8,128)(2,1)}, u32[]{:S(2)}) copy-start(bf16[256,256]{0,1:T(8,128)(2,1)} %copy.34) | copy-start | bytes 393220
  107.4 2.6 %copy-start.7 = (bf16[256,256]{1,0:T(8,128)(2,1)S(1)}, bf16[256,256]{1,0:T(8,128)(2,1)}, u32[]{:S(2)}) copy-start(bf16[256,256]{1,0:T(8,128)(2,1)} %get-tuple-element.17) | copy-start | bytes 393220
  109.8 0.7 copy-start.9
  109.9 0.7 copy-start.10
  109.9 0.7 copy-start.11
  109.9 0.7 copy-start.12
  109.9 0.7 copy-start.13
  109.9 0.7 copy-start.14
  122.5 3.8 %collective-permute-start = (bf16[160,1536]{1,0:T(8,128)(2,1)S(1)}, bf16[160,1536]{1,0:T(8,128)(2,1)S(1)}, u32[]{:S(2)}, u32[]{:S(2)}) collective-permute-start(bf16[160,1536]{1,0:T(8,128)(2,1)S(1)} %convolution_convert_fusion), channel_id=1, source_target_pairs={{0,1},{1,0},{2,3},{3,2},{4,5},{5,4},{6,7},{7,6},{8,9},{9,8},{10,11... | collective-permute-start | bytes 1474568 | tf_op jit(solution)/shard_map/ppermute | solution.py:207
  129.8 25.3 %all-to-all-start.2 = ((bf16[8,20,1536]{2,1,0:T(8,128)(2,1)}), bf16[8,20,1536]{2,1,0:T(8,128)(2,1)S(1)}, u32[]{:S(2)}, u32[]{:S(2)}) async-start(bf16[8,20,1536]{2,1,0:T(8,128)(2,1)} %reshape.255), calls=%async_computation.2 | async-start | bytes 1179648 | tf_op jit(solution)/shard_map/all_to_all | solution.py:209
  155.2 19.7 %copy-start.3 = (s32[1536,128]{1,0:T(8,128)S(1)}, s32[1536,128]{1,0:T(8,128)}, u32[]{:S(2)}) copy-start(s32[1536,128]{1,0:T(8,128)} %param.5) | copy-start | bytes 2359300
  176.0 15.2 %all-to-all-start.3 = ((f32[8,48,128]{2,1,0:T(8,128)}), f32[8,48,128]{2,1,0:T(8,128)S(1)}, u32[]{:S(2)}, u32[]{:S(2)}) async-start(f32[8,48,128]{2,1,0:T(8,128)} %select_maximum_fusion), calls=%async_computation.3 | async-start | bytes 393216 | tf_op jit(solution)/shard_map/all_to_all | solution.py:221
  207.4 12.7 %all-to-all-start.4 = ((f32[8,40,128]{2,1,0:T(8,128)}), f32[8,40,128]{2,1,0:T(8,128)S(1)}, u32[]{:S(2)}, u32[]{:S(2)}) async-start(f32[8,40,128]{2,1,0:T(8,128)} %broadcast_in_dim.125), calls=%async_computation.4 | async-start | bytes 327680 | tf_op jit(solution)/shard_map/all_to_all | solution.py:225
where the time goes:
time: 223 us; the launch traced here: 221 us
  waiting for transfers between devices  83.4 us (37%)
  starting transfers between devices  35.7 us (16%)
  blocking collectives  34.5 us (15%)
  local copies, waits for them, and re-layouts  25.3 us (11%)
  other arithmetic  20.5 us (9%)
  matrix products  20 us (9%)
    all_to_all x1, waiting for transfers between devices, shards(): chunk = jnp.sum(lax.all_to_all(payload, SAMP, 0, 0, tiled=True), axis=0)  30.3 us
    dot_general x9, matrix products, dot(): lax.dot_general(a, b, (contract, ((), ())), precision=precision, preferre...  20 us
    all_gather x1, blocking collectives, shards(): lax.all_gather(residual.astype(BF16).reshape(RIDGE * share, rows), BLK, a...  19.1 us
    all_to_all x1, waiting for transfers between devices, shards(): summed = lax.all_to_all(paired, 'y', 0, 0, tiled=True)  16.9 us
    psum x1, blocking collectives, shards(): ends = lax.psum(ends, 'x')  15.4 us
    all_to_all x1, waiting for transfers between devices, shards(): lax.all_to_all(jnp.broadcast_to(own_rows[None], (samp, *own_rows.shape)),...  14.7 us
    all_to_all x1, starting transfers between devices, shards(): chunk = jnp.sum(lax.all_to_all(payload, SAMP, 0, 0, tiled=True), axis=0)  13.3 us
    all_to_all x1, waiting for transfers between devices, shards(): ends = jnp.sum(lax.all_to_all(ends, 'z', 0, 0, tiled=True), axis=0)  11 us
  transfers between devices with their start and end apart: 6, of which 6 were waited for; matrix products, arithmetic and copies ran while one was open for 2% of the time, Pallas kernels for 0%

commit v1 on v0

--- a/solution.py
+++ b/solution.py
@@ -219,7 +219,8 @@
     squares = jnp.pad(squares, ((0, 0), (0, 7), (0, fresh_width - columns // zs)))
     ends = jnp.concatenate([raw_part.reshape(zs, columns // zs, fresh_width), squares], axis=1)
     ends = jnp.sum(lax.all_to_all(ends, "z", 0, 0, tiled=True), axis=0)
-    ends = lax.psum(ends, "x")
+    blocks = lax.all_gather(ends, "x", axis=0, tiled=False)
+    ends = blocks.sum(axis=0)
     raw, sum_sq = (ends[: columns // zs], ends[columns // zs, : columns // zs])
     scores = raw / jnp.sqrt(count * (sum_sq / count + EPS))[:, None]
     scores = lax.all_to_all(

time: 223 us -> 219 us (0.982)
  blocking collectives: 34.5 us -> 31 us
    psum x1 -> x0, blocking collectives: 15.4 us -> none  [shards(): ends = lax.psum(ends, 'x')]
    all_gather x0 -> x1, blocking collectives: none -> 11.9 us  [shards(): blocks = lax.all_gather(ends, 'x', axis=0, tiled=False)]
where the time goes in v1:
time: 219 us; the launch traced here: 217 us
  waiting for transfers between devices  83.4 us (38%)
  starting transfers between devices  35.7 us (16%)
  blocking collectives  31 us (14%)
  local copies, waits for them, and re-layouts  25.3 us (12%)
  other arithmetic  20.5 us (9%)
  matrix products  20 us (9%)
    all_to_all x1, waiting for transfers between devices, shards(): chunk = jnp.sum(lax.all_to_all(payload, SAMP, 0, 0, tiled=True), axis=0)  30.3 us
    dot_general x9, matrix products, dot(): lax.dot_general(a, b, (contract, ((), ())), precision=precision, preferre...  20 us
    all_gather x1, blocking collectives, shards(): lax.all_gather(residual.astype(BF16).reshape(RIDGE * share, rows), BLK, a...  19.1 us
    all_to_all x1, waiting for transfers between devices, shards(): summed = lax.all_to_all(paired, 'y', 0, 0, tiled=True)  16.9 us
    all_to_all x1, waiting for transfers between devices, shards(): lax.all_to_all(jnp.broadcast_to(own_rows[None], (samp, *own_rows.shape)),...  14.7 us
    all_to_all x1, starting transfers between devices, shards(): chunk = jnp.sum(lax.all_to_all(payload, SAMP, 0, 0, tiled=True), axis=0)  13.3 us
    all_gather x1, blocking collectives, shards(): blocks = lax.all_gather(ends, 'x', axis=0, tiled=False)  11.9 us
    all_to_all x1, waiting for transfers between devices, shards(): ends = jnp.sum(lax.all_to_all(ends, 'z', 0, 0, tiled=True), axis=0)  11 us
  transfers between devices with their start and end apart: 6, of which 6 were waited for; matrix products, arithmetic and copies ran while one was open for 2% of the time, Pallas kernels for 0%

profile of v1, /device:TPU:8, one launch (start us, length us, event | category | flops | bytes accessed | tf_op | source)
XLA Modules:
  0.0 217.4 jit_solution(13916827593753501115)
XLA Ops:
  0.6 2.3 %add_convert_fusion = bf16[1536,512]{1,0:T(8,128)(2,1)S(1)} fusion(s32[1536,512]{1,0:T(8,128)} %param.4), kind=kLoop, calls=%fused_computation.3 | loop fusion | flops 1572864 | bytes 4718592 | tf_op jit(solution)/shard_map/convert_element_type | solution.py:82
  3.0 1.4 fusion.2
  6.6 2.1 fusion.119
  9.8 1.3 constant_dynamic-update-slice_fusion.4
  11.1 1.3 constant_dynamic-update-slice_fusion.3
  13.6 1.3 constant_dynamic-update-slice_fusion.1
  14.9 1.3 constant_dynamic-update-slice_fusion
  16.9 1.4 maximum_bitcast_fusion
  19.4 13.3 %all-to-all-start = ((f32[32,8,1152]{2,1,0:T(8,128)}), f32[32,8,1152]{2,1,0:T(8,128)}, u32[]{:S(2)}, u32[]{:S(2)}) async-start(f32[32,8,1152]{2,1,0:T(8,128)} %pad_maximum_fusion), calls=%async_computation | async-start | bytes 2359296 | tf_op jit(solution)/shard_map/all_to_all | solution.py:108
  33.7 30.3 %all-to-all-done = f32[32,8,1152]{2,1,0:T(8,128)} async-done(((f32[32,8,1152]{2,1,0:T(8,128)}), f32[32,8,1152]{2,1,0:T(8,128)}, u32[]{:S(2)}, u32[]{:S(2)}) %all-to-all-start) | async-done | bytes 1179680 | tf_op jit(solution)/shard_map/all_to_all | solution.py:108
  64.0 2.0 reduce_sum.106
  71.6 5.3 %all-to-all-start.1 = ((bf16[32,8,1024]{2,1,0:T(8,128)(2,1)}), bf16[32,8,1024]{2,1,0:T(8,128)(2,1)}, u32[]{:S(2)}, u32[]{:S(2)}) async-start(bf16[32,8,1024]{2,1,0:T(8,128)(2,1)} %broadcast_in_dim.108), calls=%async_computation.1 | async-start | bytes 1048576 | tf_op jit(solution)/shard_map/all_to_all | solution.py:156
  78.7 14.7 %all-to-all-done.1 = bf16[32,8,1024]{2,1,0:T(8,128)(2,1)} async-done(((bf16[32,8,1024]{2,1,0:T(8,128)(2,1)}), bf16[32,8,1024]{2,1,0:T(8,128)(2,1)}, u32[]{:S(2)}, u32[]{:S(2)}) %all-to-all-start.1) | async-done | bytes 524320 | tf_op jit(solution)/shard_map/all_to_all | solution.py:156
  93.5 1.8 fusion.170
  95.3 1.7 concatenate.57
  96.9 1.7 copy.42
  100.4 1.4 fusion.150
  105.7 1.7 copy.36
  108.5 1.3 fusion.111
  110.6 11.3 %convolution_convert_fusion.1 = bf16[320,512]{1,0:T(8,128)(2,1)S(1)} fusion(f32[64,512]{1,0:T(8,128)S(1)} %fusion.109, f32[64,512]{1,0:T(8,128)S(1)} %get-tuple-element.14, f32[64,512]{1,0:T(8,128)S(1)} %get-tuple-element.20, f32[]{:T(128)} %bitcast.18, f32[]{:T(128)} %bitcast.17, f32[]{:T(128)} %bitcast.16, f32[]{:T(128)} %bitcast.15, f32[]{:T(128)} %bitcast.14, ...), kind=kOutput, calls=%fused_computation.6 | convolution fusion | flops 383008768 | bytes 726720 | tf_op jit(solution)/shard_map/dot_general | solution.py:16
  122.5 1.9 collective-permute-start
  124.5 1.8 collective-permute-done
  126.3 1.5 add_convert_fusion.1
  127.8 2.0 reshape.255
  129.8 7.5 %all-to-all-start.2 = ((bf16[8,20,1536]{2,1,0:T(8,128)(2,1)}), bf16[8,20,1536]{2,1,0:T(8,128)(2,1)S(1)}, u32[]{:S(2)}, u32[]{:S(2)}) async-start(bf16[8,20,1536]{2,1,0:T(8,128)(2,1)} %reshape.255), calls=%async_computation.2 | async-start | bytes 1179648 | tf_op jit(solution)/shard_map/all_to_all | solution.py:209
  138.1 16.9 %all-to-all-done.2 = bf16[8,20,1536]{2,1,0:T(8,128)(2,1)S(1)} async-done(((bf16[8,20,1536]{2,1,0:T(8,128)(2,1)}), bf16[8,20,1536]{2,1,0:T(8,128)(2,1)S(1)}, u32[]{:S(2)}, u32[]{:S(2)}) %all-to-all-start.2) | async-done | bytes 491552 | tf_op jit(solution)/shard_map/all_to_all | solution.py:209
  155.2 19.1 %all-gather.1 = bf16[16,20,1536]{2,1,0:T(8,128)(2,1)S(1)} all-gather(bf16[1,20,1536]{2,1,0:T(8,128)(2,1)S(1)} %fusion.121), channel_id=1, replica_groups=mesh['x'=4,'z'=8,'y'=8,'core'=2] {'y','core'}, dimensions={0}, use_global_device_ids=true | all-gather | bytes 1044480 | tf_op jit(solution)/shard_map/all_gather | solution.py:213
  176.0 4.2 %all-to-all-start.3 = ((f32[8,48,128]{2,1,0:T(8,128)}), f32[8,48,128]{2,1,0:T(8,128)S(1)}, u32[]{:S(2)}, u32[]{:S(2)}) async-start(f32[8,48,128]{2,1,0:T(8,128)} %select_maximum_fusion), calls=%async_computation.3 | async-start | bytes 393216 | tf_op jit(solution)/shard_map/all_to_all | solution.py:221
  180.3 11.0 %all-to-all-done.3 = f32[8,48,128]{2,1,0:T(8,128)S(1)} async-done(((f32[8,48,128]{2,1,0:T(8,128)}), f32[8,48,128]{2,1,0:T(8,128)S(1)}, u32[]{:S(2)}, u32[]{:S(2)}) %all-to-all-start.3) | async-done | bytes 196640 | tf_op jit(solution)/shard_map/all_to_all | solution.py:221
  191.3 11.9 %all-gather = f32[192,128]{1,0:T(8,128)S(1)} all-gather(f32[48,128]{1,0:T(8,128)S(1)} %reduce_sum.111), channel_id=2, replica_groups=mesh['x'=4,'z'=8,'y'=8,'core'=2] {'x'}, dimensions={0}, use_global_device_ids=true | all-gather | bytes 122880 | tf_op jit(solution)/shard_map/all_gather | solution.py:222
  204.0 3.4 %all-to-all-start.4 = ((f32[8,40,128]{2,1,0:T(8,128)}), f32[8,40,128]{2,1,0:T(8,128)S(1)}, u32[]{:S(2)}, u32[]{:S(2)}) async-start(f32[8,40,128]{2,1,0:T(8,128)} %broadcast_in_dim.125), calls=%async_computation.4 | async-start | bytes 327680 | tf_op jit(solution)/shard_map/all_to_all | solution.py:226
  208.0 8.7 %all-to-all-done.4 = f32[8,40,128]{2,1,0:T(8,128)S(1)} async-done(((f32[8,40,128]{2,1,0:T(8,128)}), f32[8,40,128]{2,1,0:T(8,128)S(1)}, u32[]{:S(2)}, u32[]{:S(2)}) %all-to-all-start.4) | async-done | bytes 163872 | tf_op jit(solution)/shard_map/all_to_all | solution.py:226
  (100 shorter events, 27.3 us)
Async XLA Ops:
  3.0 2.5 %copy-start.1 = (bf16[1536,512]{1,0:T(8,128)(2,1)}, bf16[1536,512]{1,0:T(8,128)(2,1)S(1)}, u32[]{:S(2)}) copy-start(bf16[1536,512]{1,0:T(8,128)(2,1)S(1)} %add_convert_fusion) | copy-start | bytes 4718596
  3.0 2.6 %copy-start = (s32[1536,512]{1,0:T(8,128)S(1)}, s32[1536,512]{1,0:T(8,128)}, u32[]{:S(2)}) copy-start(s32[1536,512]{1,0:T(8,128)} %param.4) | copy-start | bytes 9437188
  5.6 1.0 copy-start.4
  6.6 2.9 %copy-start.2 = (s32[1536,128]{1,0:T(8,128)S(1)}, s32[1536,128]{1,0:T(8,128)}, u32[]{:S(2)}) copy-start(s32[1536,128]{1,0:T(8,128)} %param.5) | copy-start | bytes 2359300
  19.4 44.6 %all-to-all-start = ((f32[32,8,1152]{2,1,0:T(8,128)}), f32[32,8,1152]{2,1,0:T(8,128)}, u32[]{:S(2)}, u32[]{:S(2)}) async-start(f32[32,8,1152]{2,1,0:T(8,128)} %pad_maximum_fusion), calls=%async_computation | async-start | bytes 2359296 | tf_op jit(solution)/shard_map/all_to_all | solution.py:108
  68.5 0.6 copy-start.8
  71.6 21.8 %all-to-all-start.1 = ((bf16[32,8,1024]{2,1,0:T(8,128)(2,1)}), bf16[32,8,1024]{2,1,0:T(8,128)(2,1)}, u32[]{:S(2)}, u32[]{:S(2)}) async-start(bf16[32,8,1024]{2,1,0:T(8,128)(2,1)} %broadcast_in_dim.108), calls=%async_computation.1 | async-start | bytes 1048576 | tf_op jit(solution)/shard_map/all_to_all | solution.py:156
  107.4 2.6 %copy-start.5 = (bf16[256,512]{1,0:T(8,128)(2,1)S(1)}, bf16[256,512]{1,0:T(8,128)(2,1)}, u32[]{:S(2)}) copy-start(bf16[256,512]{1,0:T(8,128)(2,1)} %concatenate.57) | copy-start | bytes 786436
  107.4 2.6 %copy-start.6 = (bf16[256,256]{0,1:T(8,128)(2,1)S(1)}, bf16[256,256]{0,1:T(8,128)(2,1)}, u32[]{:S(2)}) copy-start(bf16[256,256]{0,1:T(8,128)(2,1)} %copy.42) | copy-start | bytes 393220
  107.4 2.6 %copy-start.7 = (bf16[256,256]{1,0:T(8,128)(2,1)S(1)}, bf16[256,256]{1,0:T(8,128)(2,1)}, u32[]{:S(2)}) copy-start(bf16[256,256]{1,0:T(8,128)(2,1)} %get-tuple-element.17) | copy-start | bytes 393220
  109.8 0.7 copy-start.9
  109.9 0.7 copy-start.10
  109.9 0.7 copy-start.11
  109.9 0.7 copy-start.12
  109.9 0.7 copy-start.13
  109.9 0.7 copy-start.14
  122.5 3.8 %collective-permute-start = (bf16[160,1536]{1,0:T(8,128)(2,1)S(1)}, bf16[160,1536]{1,0:T(8,128)(2,1)S(1)}, u32[]{:S(2)}, u32[]{:S(2)}) collective-permute-start(bf16[160,1536]{1,0:T(8,128)(2,1)S(1)} %convolution_convert_fusion), channel_id=1, source_target_pairs={{0,1},{1,0},{2,3},{3,2},{4,5},{5,4},{6,7},{7,6},{8,9},{9,8},{10,11... | collective-permute-start | bytes 1474568 | tf_op jit(solution)/shard_map/ppermute | solution.py:207
  129.8 25.3 %all-to-all-start.2 = ((bf16[8,20,1536]{2,1,0:T(8,128)(2,1)}), bf16[8,20,1536]{2,1,0:T(8,128)(2,1)S(1)}, u32[]{:S(2)}, u32[]{:S(2)}) async-start(bf16[8,20,1536]{2,1,0:T(8,128)(2,1)} %reshape.255), calls=%async_computation.2 | async-start | bytes 1179648 | tf_op jit(solution)/shard_map/all_to_all | solution.py:209
  155.2 19.7 %copy-start.3 = (s32[1536,128]{1,0:T(8,128)S(1)}, s32[1536,128]{1,0:T(8,128)}, u32[]{:S(2)}) copy-start(s32[1536,128]{1,0:T(8,128)} %param.5) | copy-start | bytes 2359300
  176.0 15.2 %all-to-all-start.3 = ((f32[8,48,128]{2,1,0:T(8,128)}), f32[8,48,128]{2,1,0:T(8,128)S(1)}, u32[]{:S(2)}, u32[]{:S(2)}) async-start(f32[8,48,128]{2,1,0:T(8,128)} %select_maximum_fusion), calls=%async_computation.3 | async-start | bytes 393216 | tf_op jit(solution)/shard_map/all_to_all | solution.py:221
  204.0 12.7 %all-to-all-start.4 = ((f32[8,40,128]{2,1,0:T(8,128)}), f32[8,40,128]{2,1,0:T(8,128)S(1)}, u32[]{:S(2)}, u32[]{:S(2)}) async-start(f32[8,40,128]{2,1,0:T(8,128)} %broadcast_in_dim.125), calls=%async_computation.4 | async-start | bytes 327680 | tf_op jit(solution)/shard_map/all_to_all | solution.py:226
